TPU v7x, 32 devices: a whole 2x2x4 slice. The times are simulated.
32 devices in a mesh: row: 4 (over x, core), col: 8 (over z, y).
Axes of the slice: x: 2, y: 2, z: 4, core: 2. Of those that a mesh axis runs over, the one named last changes fastest.
Arguments:
- amplitudes: bfloat16 [640, 90000], P(('row', 'col')), may hold values from -6 to 6
- coulomb: bfloat16 [90000, 8192], P('col', 'row'), may hold values from -0.01953125 to 0.01953125
Outputs:
- ladder: float32 [640, 8192], P('col', 'row')
All inputs are finite; a program needn't handle non-finite values.
Results may differ from a plain program's by a relative error of at most 0.0003.
Values may be sent and summed in bfloat16 or wider, within the bound.
A program may use at most 192 MiB of HBM per device.

v0:
```python
import jax
import jax.numpy as jnp
from jax import lax
from jax.sharding import PartitionSpec as P


def shards(amplitudes, coulomb):
    columns = lax.axis_size("col")
    grid_rows = lax.axis_size("row")
    pairs_here = amplitudes.shape[0]
    gathered = lax.all_gather(amplitudes, "row", axis=0, tiled=True)
    divided = lax.all_to_all(gathered, "col", split_axis=1, concat_axis=0, tiled=True)
    amp_panel = (
        divided.reshape(columns, grid_rows, pairs_here, -1)
        .transpose(1, 0, 2, 3)
        .reshape(columns * grid_rows * pairs_here, -1)
    )
    contraction = lax.psum_scatter(
        jnp.dot(amp_panel, coulomb, preferred_element_type=jnp.float32),
        "col",
        scatter_dimension=0,
        tiled=True,
    )
    return 0.5 * contraction


def solution(mesh):
    return jax.shard_map(
        shards,
        mesh=mesh,
        in_specs=(P(("row", "col"), None), P("col", "row")),
        out_specs=P("col", "row"),
        check_vma=False,
    )
```

profile of v0, /device:TPU:0, one launch (start us, length us, event | category | flops | bytes accessed | tf_op | source)
XLA Modules:
  0.0 709.9 jit_solution(15192235803599281325)
XLA Ops:
  6.5 0.0 all-gather.3.cloned.1.call-start
  6.5 0.7 all-gather.3.cloned.1.call-update
  7.3 0.0 reduce-scatter.2.cloned.1.call-start
  7.3 115.6 %all-gather.3.cloned.1.call-done = bf16[4,20,90000]{2,1,0:T(8,128)(2,1)} async-done(((bf16[1,20,90000]{2,1,0:T(8,128)(2,1)}), bf16[4,20,90000]{2,1,0:T(8,128)(2,1)}) %all-gather.3.cloned.1.call-update) | async-done | bytes 14400016 | tf_op jit(solution)/shard_map/all_gather | solution.py:11
  122.9 39.6 %all_to_all.12 = bf16[80,8,11250]{2,1,0:T(8,128)(2,1)} reshape(bf16[4,20,90000]{2,1,0:T(8,128)(2,1)} %all-gather.3.cloned.1.call-done) | data formatting | bytes 28800000 | tf_op jit(solution)/shard_map/all_to_all | solution.py:12
  162.6 9.2 %copy.6 = bf16[80,8,11250]{2,0,1:T(8,128)(2,1)S(1)} copy(bf16[80,8,11250]{2,1,0:T(8,128)(2,1)} %all_to_all.12) | data formatting | bytes 28800000 | tf_op jit(solution)/shard_map/all_to_all | solution.py:12
  171.8 318.0 %all_to_all.16 = bf16[80,8,11250]{2,0,1:T(8,128)(2,1)S(1)} all-to-all(bf16[80,8,11250]{2,0,1:T(8,128)(2,1)S(1)} %copy.6), channel_id=1, replica_groups=mesh['row'=4,'col'=8] {'col'}, dimensions={1} | all-to-all | bytes 28800000 | tf_op jit(solution)/shard_map/all_to_all | solution.py:12
  489.8 29.1 %copy.7 = bf16[80,8,11250]{2,1,0:T(8,128)(2,1)S(1)} copy(bf16[80,8,11250]{2,0,1:T(8,128)(2,1)S(1)} %all_to_all.16) | data formatting | bytes 28800000 | tf_op jit(solution)/shard_map/all_to_all | solution.py:12
  518.8 23.8 %copy.8 = bf16[4,8,20,11250]{3,2,1,0:T(8,128)(2,1)} copy(bf16[4,8,20,11250]{3,1,2,0:T(8,128)(2,1)S(1)} %bitcast.8) | data formatting | bytes 28800000 | tf_op jit(solution)/shard_map/transpose | solution.py:15
  542.7 19.0 %reshape.11 = bf16[640,11250]{1,0:T(8,128)(2,1)} reshape(bf16[4,8,20,11250]{3,2,1,0:T(8,128)(2,1)} %copy.8) | data formatting | bytes 28800000 | tf_op jit(solution)/shard_map/reshape | solution.py:16
  561.7 38.1 %fusion = f32[640,2048]{1,0:T(8,128)} fusion(bf16[640,11250]{1,0:T(8,128)(2,1)} %reshape.11, bf16[11250,2048]{1,0:T(8,128)(2,1)} %param.3), kind=kOutput, calls=%fused_computation.1 | convolution fusion | flops 29491200000 | bytes 65722880 | tf_op jit(solution)/shard_map/dot_general | solution.py:19
  599.8 0.0 reduce-scatter.2.cloned.1.call-update
  599.8 101.3 %reduce-scatter.2.cloned.1.call-done = f32[80,2048]{1,0:T(8,128)} async-done(((f32[640,2048]{1,0:T(8,128)}), f32[80,2048]{1,0:T(8,128)}) %reduce-scatter.2.cloned.1.call-update) | async-done | bytes 655376 | tf_op jit(solution)/shard_map/reduce_scatter | solution.py:18
  701.1 2.0 broadcast_multiply_fusion
Async XLA Ops:
  6.5 116.4 %all-gather.3.cloned.1.call-start = ((), (), s32[]{:S(2)}) async-start(), calls=%async_computation.3 | async-start | bytes 21626880 | tf_op jit(solution)/shard_map/all_gather | solution.py:11
  7.3 693.8 %reduce-scatter.2.cloned.1.call-start = ((), (), s32[]{:S(2)}) async-start(), calls=%async_computation.2 | async-start | bytes 5898240 | tf_op jit(solution)/shard_map/reduce_scatter | solution.py:18
Sparse Core Ops, SparseCore 0:
  8.9 113.9 all-gather.2
  599.9 101.1 reduce-scatter.1
where the time goes:
time: 711 us; the launch traced here: 710 us
  blocking collectives  318 us (45%)
  waiting for transfers between devices  218 us (31%)
  local copies, waits for them, and re-layouts  121 us (17%)
  matrix products  38.1 us (5%)
  between operations  13.4 us (2%)
    all_to_all x1, blocking collectives, shards(): lax.all_to_all(gathered, 'col', split_axis=1, concat_axis=0, tiled=True)  318 us
    all_gather x1, waiting for transfers between devices, shards(): gathered = lax.all_gather(amplitudes, 'row', axis=0, tiled=True)  116 us
    reduce_scatter x1, waiting for transfers between devices, shards(): lax.psum_scatter(jnp.dot(amp_panel, coulomb, preferred_element_type=jnp.f...  101 us
    all_to_all x3, local copies, waits for them, and re-layouts, shards(): lax.all_to_all(gathered, 'col', split_axis=1, concat_axis=0, tiled=True)  77.9 us
    dot_general x1, matrix products, shards(): jnp.dot(amp_panel, coulomb, preferred_element_type=jnp.float32)  38.1 us
    transpose x1, local copies, waits for them, and re-layouts, shards(): amp_panel = divided.reshape(columns, grid_rows, pairs_here, -1).transpose...  23.8 us
    reshape x1, local copies, waits for them, and re-layouts, shards(): amp_panel = divided.reshape(columns, grid_rows, pairs_here, -1).transpose...  19 us
  transfers between devices with their start and end apart: 2, of which 2 were waited for; matrix products, arithmetic and copies ran while one was open for 0% of the time, Pallas kernels for 0%

commit v1 on v0

--- a/solution.py
+++ b/solution.py
@@ -8,13 +8,10 @@
     columns = lax.axis_size("col")
     grid_rows = lax.axis_size("row")
     pairs_here = amplitudes.shape[0]
-    gathered = lax.all_gather(amplitudes, "row", axis=0, tiled=True)
-    divided = lax.all_to_all(gathered, "col", split_axis=1, concat_axis=0, tiled=True)
-    amp_panel = (
-        divided.reshape(columns, grid_rows, pairs_here, -1)
-        .transpose(1, 0, 2, 3)
-        .reshape(columns * grid_rows * pairs_here, -1)
-    )
+    blocks = amplitudes.reshape(pairs_here, columns, -1).transpose(1, 0, 2)
+    mine = lax.all_to_all(blocks, "col", split_axis=0, concat_axis=0, tiled=True)
+    mine = mine.reshape(columns * pairs_here, -1)
+    amp_panel = lax.all_gather(mine, "row", axis=0, tiled=True)
     contraction = lax.psum_scatter(
         jnp.dot(amp_panel, coulomb, preferred_element_type=jnp.float32),
         "col",

time: 711 us -> 369 us (0.52)
  blocking collectives: 318 us -> 104 us
  local copies, waits for them, and re-layouts: 121 us -> 16.9 us
  waiting for transfers between devices: 218 us -> 194 us
    all_to_all x1, blocking collectives: 318 us -> 104 us  [shards(): lax.all_to_all(blocks, 'col', split_axis=0, concat_axis=0, tiled=True)]
    all_to_all x3 -> x0, local copies, waits for them, and re-layouts: 77.9 us -> none  [shards(): lax.all_to_all(gathered, 'col', split_axis=1, concat_axis=0, tiled=True)]
    all_gather x1, waiting for transfers between devices: 116 us -> 91.3 us  [shards(): amp_panel = lax.all_gather(mine, 'row', axis=0, tiled=True)]
    transpose x1 -> x0, local copies, waits for them, and re-layouts: 23.8 us -> none  [shards(): amp_panel = divided.reshape(columns, grid_rows, pairs_here, -1).transpose...]
    reshape x1 -> x3, local copies, waits for them, and re-layouts: 19 us -> 16.9 us  [the longest x2 11.6 us: shards(): blocks = amplitudes.reshape(pairs_here, columns, -1).transpose(1, 0, 2)]
where the time goes in v1:
time: 369 us; the launch traced here: 368 us
  waiting for transfers between devices  194 us (53%)
  blocking collectives  104 us (28%)
  matrix products  38.1 us (10%)
  local copies, waits for them, and re-layouts  16.9 us (5%)
  between operations  13.4 us (4%)
    all_to_all x1, blocking collectives, shards(): lax.all_to_all(blocks, 'col', split_axis=0, concat_axis=0, tiled=True)  104 us
    reduce_scatter x1, waiting for transfers between devices, shards(): lax.psum_scatter(jnp.dot(amp_panel, coulomb, preferred_element_type=jnp.f...  103 us
    all_gather x1, waiting for transfers between devices, shards(): amp_panel = lax.all_gather(mine, 'row', axis=0, tiled=True)  91.3 us
    dot_general x1, matrix products, shards(): jnp.dot(amp_panel, coulomb, preferred_element_type=jnp.float32)  38.1 us
    reshape x2, local copies, waits for them, and re-layouts, shards(): blocks = amplitudes.reshape(pairs_here, columns, -1).transpose(1, 0, 2)  11.6 us
  transfers between devices with their start and end apart: 2, of which 2 were waited for; matrix products, arithmetic and copies ran while one was open for 0% of the time, Pallas kernels for 0%

profile of v1, /device:TPU:0, one launch (start us, length us, event | category | flops | bytes accessed | tf_op | source)
XLA Modules:
  0.0 368.4 jit_solution(8066125965963623343)
XLA Ops:
  6.5 0.0 all-gather.2.cloned.1.call-start
  6.5 7.6 %reshape.6 = bf16[20,8,11250]{2,1,0:T(8,128)(2,1)} reshape(bf16[20,90000]{1,0:T(8,128)(2,1)} %param.2) | data formatting | bytes 7200000 | tf_op jit(solution)/shard_map/reshape | solution.py:11
  14.1 4.0 %copy.5 = bf16[20,8,11250]{2,0,1:T(8,128)(2,1)S(1)} copy(bf16[20,8,11250]{2,1,0:T(8,128)(2,1)} %reshape.6) | data formatting | bytes 7200000 | tf_op jit(solution)/shard_map/reshape | solution.py:11
  18.1 103.5 %all_to_all.5 = bf16[8,20,11250]{2,1,0:T(8,128)(2,1)} all-to-all(bf16[8,20,11250]{2,1,0:T(8,128)(2,1)S(1)} %bitcast.5), channel_id=1, replica_groups=mesh['row'=4,'col'=8] {'col'}, dimensions={0} | all-to-all | bytes 7200000 | tf_op jit(solution)/shard_map/all_to_all | solution.py:12
  121.7 5.3 %reshape.7 = bf16[160,11250]{1,0:T(8,128)(2,1)} reshape(bf16[8,20,11250]{2,1,0:T(8,128)(2,1)} %all_to_all.5) | data formatting | bytes 7200000 | tf_op jit(solution)/shard_map/reshape | solution.py:13
  127.0 0.0 all-gather.2.cloned.1.call-update
  127.0 0.0 reduce-scatter.2.cloned.1.call-start
  127.0 91.3 %all-gather.2.cloned.1.call-done = bf16[640,11250]{1,0:T(8,128)(2,1)} async-done(((bf16[160,11250]{1,0:T(8,128)(2,1)}), bf16[640,11250]{1,0:T(8,128)(2,1)}) %all-gather.2.cloned.1.call-update) | async-done | bytes 14400016 | tf_op jit(solution)/shard_map/all_gather | solution.py:14
  218.3 38.1 %fusion = f32[640,2048]{1,0:T(8,128)} fusion(bf16[640,11250]{1,0:T(8,128)(2,1)} %all-gather.2.cloned.1.call-done, bf16[11250,2048]{1,0:T(8,128)(2,1)} %param.3), kind=kOutput, calls=%fused_computation.2 | convolution fusion | flops 29491200000 | bytes 65722880 | tf_op jit(solution)/shard_map/dot_general | solution.py:16
  256.4 0.0 reduce-scatter.2.cloned.1.call-update
  256.4 103.2 %reduce-scatter.2.cloned.1.call-done = f32[80,2048]{1,0:T(8,128)} async-done(((f32[640,2048]{1,0:T(8,128)}), f32[80,2048]{1,0:T(8,128)}) %reduce-scatter.2.cloned.1.call-update) | async-done | bytes 655376 | tf_op jit(solution)/shard_map/reduce_scatter | solution.py:15
  359.6 2.0 broadcast_multiply_fusion
Async XLA Ops:
  6.5 211.8 %all-gather.2.cloned.1.call-start = ((), (), s32[]{:S(2)}) async-start(), calls=%async_computation.2 | async-start | bytes 18022400 | tf_op jit(solution)/shard_map/all_gather | solution.py:14
  127.0 232.6 %reduce-scatter.2.cloned.1.call-start = ((), (), s32[]{:S(2)}) async-start(), calls=%async_computation.3 | async-start | bytes 5898240 | tf_op jit(solution)/shard_map/reduce_scatter | solution.py:15
Sparse Core Ops, SparseCore 0:
  127.1 91.1 all-gather.1
  256.5 102.9 reduce-scatter.1

commit v2 on v1

v2 whole, which is shorter than its diff:
```python
import jax
import jax.numpy as jnp
from jax import lax
from jax.sharding import PartitionSpec as P


CD_CHUNKS = 3
AB_CHUNKS = 2
LANES = 128


def cuts(length, parts, unit):
    step = -(-(-(-length // unit)) // parts) * unit
    return [(at, min(at + step, length)) for at in range(0, length, step)]


def shards(amplitudes, coulomb):
    columns = lax.axis_size("col")
    pairs_here = amplitudes.shape[0]
    blocks = amplitudes.reshape(pairs_here, columns, -1).transpose(1, 0, 2)
    cd_cuts = cuts(coulomb.shape[0], CD_CHUNKS, LANES)
    ab_cuts = cuts(coulomb.shape[1], AB_CHUNKS, LANES)
    totals = [None] * len(ab_cuts)
    token = None
    for low, high in cd_cuts:
        piece = blocks[:, :, low:high]
        if token is not None:
            piece, token = lax.optimization_barrier((piece, token))
        mine = lax.all_to_all(piece, "col", split_axis=0, concat_axis=0, tiled=True)
        mine = mine.reshape(columns * pairs_here, -1)
        token = mine
        panel = lax.all_gather(mine, "row", axis=0, tiled=True)
        for at, (left, right) in enumerate(ab_cuts):
            term = jnp.dot(panel, coulomb[low:high, left:right], preferred_element_type=jnp.float32)
            total = term if totals[at] is None else totals[at] + term
            totals[at] = lax.optimization_barrier(total)
    out = [
        lax.psum_scatter(total, "col", scatter_dimension=0, tiled=True)
        for total in totals
    ]
    return 0.5 * jnp.concatenate(out, axis=1)


def solution(mesh):
    return jax.shard_map(
        shards,
        mesh=mesh,
        in_specs=(P(("row", "col"), None), P("col", "row")),
        out_specs=P("col", "row"),
        check_vma=False,
    )
```

time: 369 us -> 344 us (0.932)
  waiting for transfers between devices: 194 us -> 134 us
  matrix products: 38.1 us -> 58.5 us
  blocking collectives: 104 us -> 117 us
    all_gather x1 -> x3, waiting for transfers between devices: 91.3 us -> 17.6 us  [shards(): panel = lax.all_gather(mine, 'row', axis=0, tiled=True)]
    dot_general x1 -> x6, matrix products: 38.1 us -> 58.5 us  [shards(): jnp.dot(panel, coulomb[low:high, left:right], preferred_element_type=jnp....]
    reduce_scatter x1 -> x2, waiting for transfers between devices: 103 us -> 116 us  [shards(): lax.psum_scatter(total, 'col', scatter_dimension=0, tiled=True)]
    all_to_all x1 -> x3, blocking collectives: 104 us -> 117 us  [shards(): mine = lax.all_to_all(piece, 'col', split_axis=0, concat_axis=0, tiled=True)]
  transfers between devices with their start and end apart: 2 -> 5, of which waited for: 2 -> 3; matrix products, arithmetic and copies ran while one was open for 0% -> 15% of each run, Pallas kernels for 0% -> 0%
where the time goes in v2:
time: 344 us
  waiting for transfers between devices  134 us (39%)
  blocking collectives  117 us (34%)
  matrix products  58.5 us (17%)
  local copies, waits for them, and re-layouts  19 us (6%)
  between operations  13.2 us (4%)
    all_to_all x3, blocking collectives, shards(): mine = lax.all_to_all(piece, 'col', split_axis=0, concat_axis=0, tiled=True)  117 us
    reduce_scatter x2, waiting for transfers between devices, shards(): lax.psum_scatter(total, 'col', scatter_dimension=0, tiled=True)  116 us
    dot_general x6, matrix products, shards(): jnp.dot(panel, coulomb[low:high, left:right], preferred_element_type=jnp....  58.5 us
    all_gather x3, waiting for transfers between devices, shards(): panel = lax.all_gather(mine, 'row', axis=0, tiled=True)  17.6 us
    reshape x2, local copies, waits for them, and re-layouts, shards(): blocks = amplitudes.reshape(pairs_here, columns, -1).transpose(1, 0, 2)  11.6 us
  transfers between devices with their start and end apart: 5, of which 3 were waited for; matrix products, arithmetic and copies ran while one was open for 15% of the time, Pallas kernels for 0%

profile of v2, /device:TPU:0, one launch (start us, length us, event | category | flops | bytes accessed | tf_op | source)
XLA Modules:
  0.0 343.7 jit_solution(3792869997107065315)
XLA Ops:
  6.5 0.0 all-gather.4.cloned.1.call-start
  6.5 7.6 %reshape.12 = bf16[20,8,11250]{2,1,0:T(8,128)(2,1)} reshape(bf16[20,90000]{1,0:T(8,128)(2,1)} %param.2) | data formatting | bytes 7200000 | tf_op jit(solution)/shard_map/reshape | solution.py:20
  14.1 4.0 %copy.5 = bf16[20,8,11250]{2,0,1:T(8,128)(2,1)S(1)} copy(bf16[20,8,11250]{2,1,0:T(8,128)(2,1)} %reshape.12) | data formatting | bytes 7200000 | tf_op jit(solution)/shard_map/reshape | solution.py:20
  18.2 0.0 copy-start
  18.2 2.1 copy-done
  20.3 0.2 fusion.24
  20.5 42.2 %all_to_all.15 = bf16[8,20,3840]{2,1,0:T(8,128)(2,1)S(1)} all-to-all(bf16[8,20,3840]{2,1,0:T(8,128)(2,1)S(1)} %get-tuple-element.10), channel_id=1, replica_groups=mesh['row'=4,'col'=8] {'col'}, dimensions={0} | all-to-all | bytes 2457600 | tf_op jit(solution)/shard_map/all_to_all | solution.py:29
  62.7 1.2 reshape.13
  63.8 0.0 all-gather.4.cloned.1.call-update
  63.9 0.0 all-gather.6.cloned.1.call-start
  63.9 38.1 %all_to_all.16 = bf16[8,20,3840]{2,1,0:T(8,128)(2,1)S(1)} all-to-all(bf16[8,20,3840]{2,1,0:T(8,128)(2,1)S(1)} %get-tuple-element.7), channel_id=1, replica_groups=mesh['row'=4,'col'=8] {'col'}, dimensions={0} | all-to-all | bytes 2457600 | tf_op jit(solution)/shard_map/all_to_all | solution.py:29
  102.0 1.2 reshape.14
  103.2 0.0 all-gather.6.cloned.1.call-update
  103.2 0.0 all-gather.8.cloned.1.call-start
  103.3 1.4 slice.38
  104.7 36.3 %all_to_all.17 = bf16[8,20,3570]{2,1,0:T(8,128)(2,1)S(1)} all-to-all(bf16[8,20,3570]{2,1,0:T(8,128)(2,1)S(1)} %slice.38), channel_id=1, replica_groups=mesh['row'=4,'col'=8] {'col'}, dimensions={0} | all-to-all | bytes 2284800 | tf_op jit(solution)/shard_map/all_to_all | solution.py:29
  141.0 1.3 reshape.15
  142.3 0.0 all-gather.8.cloned.1.call-update
  142.4 0.2 reduce-scatter.5.cloned.1.call-start
  142.6 0.0 all-gather.4.cloned.1.call-done
  142.6 10.1 %fusion.2 = f32[640,1024]{1,0:T(8,128)} fusion(bf16[640,3840]{1,0:T(8,128)(2,1)} %all-gather.4.cloned.1.call-done, bf16[11250,2048]{1,0:T(8,128)(2,1)} %param.3), kind=kOutput, calls=%fused_computation.2 | convolution fusion | flops 5033164800 | bytes 15400960 | tf_op jit(solution)/shard_map/dot_general | solution.py:34
  152.7 0.0 all-gather.6.cloned.1.call-done
  152.7 9.5 %fusion.15 = f32[640,1024]{1,0:T(8,128)S(1)} fusion(f32[640,1024]{1,0:T(8,128)} %fusion.2, bf16[640,3840]{1,0:T(8,128)(2,1)} %all-gather.6.cloned.1.call-done, bf16[11250,2048]{1,0:T(8,128)(2,1)} %param.3), kind=kOutput, calls=%fused_computation.14 | convolution fusion | flops 5033820160 | bytes 18022400 | tf_op jit(solution)/shard_map/dot_general | solution.py:34
  162.2 17.6 %all-gather.8.cloned.1.call-done = bf16[640,3570]{1,0:T(8,128)(2,1)} async-done(((bf16[160,3570]{1,0:T(8,128)(2,1)}), bf16[640,3570]{1,0:T(8,128)(2,1)}) %all-gather.8.cloned.1.call-update) | async-done | bytes 4569616 | tf_op jit(solution)/shard_map/all_gather | solution.py:32
  179.8 10.8 %fusion.21 = f32[640,1024]{1,0:T(8,128)} fusion(f32[640,1024]{1,0:T(8,128)S(1)} %fusion.15, bf16[640,3570]{1,0:T(8,128)(2,1)} %all-gather.8.cloned.1.call-done, bf16[11250,2048]{1,0:T(8,128)(2,1)} %param.3), kind=kOutput, calls=%fused_computation.16 | convolution fusion | flops 4679925760 | bytes 17154048 | tf_op jit(solution)/shard_map/dot_general | solution.py:34
  190.6 0.0 reduce-scatter.5.cloned.1.call-update
  190.7 0.0 reduce-scatter.3.cloned.1.call-start
  190.7 0.0 slice-start
  190.7 9.2 %fusion.6 = f32[640,1024]{1,0:T(8,128)S(1)} fusion(bf16[640,3840]{1,0:T(8,128)(2,1)} %all-gather.4.cloned.1.call-done, bf16[11250,2048]{1,0:T(8,128)(2,1)} %param.3), kind=kOutput, calls=%fused_computation.6 | convolution fusion | flops 5033164800 | bytes 15400960 | tf_op jit(solution)/shard_map/dot_general | solution.py:34
  199.9 0.0 slice-start.1
  199.9 9.1 %fusion.12 = f32[640,1024]{1,0:T(8,128)S(1)} fusion(f32[640,1024]{1,0:T(8,128)S(1)} %fusion.6, bf16[640,3840]{1,0:T(8,128)(2,1)} %all-gather.6.cloned.1.call-done, bf16[11250,2048]{1,0:T(8,128)(2,1)} %param.3), kind=kOutput, calls=%fused_computation.13 | convolution fusion | flops 5033820160 | bytes 18022400 | tf_op jit(solution)/shard_map/dot_general | solution.py:34
  209.0 0.0 slice-done
  209.0 0.0 slice-done.1
  209.1 9.7 %fusion.18 = f32[640,1024]{1,0:T(8,128)} fusion(f32[640,1024]{1,0:T(8,128)S(1)} %fusion.12, bf16[640,3570]{1,0:T(8,128)(2,1)S(1)} %bitcast.12, bf16[11250,2048]{1,0:T(8,128)(2,1)} %param.3), kind=kOutput, calls=%fused_computation.15 | convolution fusion | flops 4679925760 | bytes 17136128 | tf_op jit(solution)/shard_map/dot_general | solution.py:34
  218.8 0.0 reduce-scatter.3.cloned.1.call-update
  218.8 42.9 %reduce-scatter.5.cloned.1.call-done = f32[80,1024]{1,0:T(8,128)} async-done(((f32[640,1024]{1,0:T(8,128)}), f32[80,1024]{1,0:T(8,128)}) %reduce-scatter.5.cloned.1.call-update) | async-done | bytes 327696 | tf_op jit(solution)/shard_map/reduce_scatter | solution.py:38
  261.7 73.5 %reduce-scatter.3.cloned.1.call-done = f32[80,1024]{1,0:T(8,128)} async-done(((f32[640,1024]{1,0:T(8,128)}), f32[80,1024]{1,0:T(8,128)}) %reduce-scatter.3.cloned.1.call-update) | async-done | bytes 327696 | tf_op jit(solution)/shard_map/reduce_scatter | solution.py:38
  335.2 2.0 maximum_multiply_fusion
  (1 shorter events, 0.0 us)
Async XLA Ops:
  6.5 136.1 %all-gather.4.cloned.1.call-start = ((), (), s32[]{:S(2)}) async-start(), calls=%async_computation.5 | async-start | bytes 6144000 | tf_op jit(solution)/shard_map/all_gather | solution.py:32
  18.2 2.1 copy-start
  63.9 88.9 %all-gather.6.cloned.1.call-start = ((), (), s32[]{:S(2)}) async-start(), calls=%async_computation.6 | async-start | bytes 6144000 | tf_op jit(solution)/shard_map/all_gather | solution.py:32
  103.2 76.6 %all-gather.8.cloned.1.call-start = ((), (), s32[]{:S(2)}) async-start(), calls=%async_computation.7 | async-start | bytes 5734400 | tf_op jit(solution)/shard_map/all_gather | solution.py:32
  142.4 119.3 %reduce-scatter.5.cloned.1.call-start = ((), (), s32[]{:S(2)}) async-start(), calls=%async_computation.9 | async-start | bytes 2949120 | tf_op jit(solution)/shard_map/reduce_scatter | solution.py:38
  190.7 144.5 %reduce-scatter.3.cloned.1.call-start = ((), (), s32[]{:S(2)}) async-start(), calls=%async_computation.8 | async-start | bytes 2949120 | tf_op jit(solution)/shard_map/reduce_scatter | solution.py:38
  190.7 18.3 %slice-start = ((s8[4587520]{0:T(1024)(128)(4,1)}), s8[4194304]{0:T(1024)(128)(4,1)S(1)}, s32[]{:S(2)}) async-start(s8[4587520]{0:T(1024)(128)(4,1)} %bitcast.11), calls=%async_computation.10 | async-start | bytes 8388608
  199.9 9.1 %slice-start.1 = ((s8[4587520]{0:T(1024)(128)(4,1)}), s8[393216]{0:T(1024)(128)(4,1)S(1)}, s32[]{:S(2)}) async-start(s8[4587520]{0:T(1024)(128)(4,1)} %bitcast.11), calls=%async_computation.11 | async-start | bytes 786432
Sparse Core Ops, SparseCore 0:
  64.0 37.3 all-gather.3
  103.3 38.1 all-gather.5
  143.1 36.6 all-gather.7
  190.8 70.8 reduce-scatter.4
  265.0 70.1 reduce-scatter.2

commit v3 on v2

v3 whole, which is shorter than its diff:
```python
import jax
import jax.numpy as jnp
from jax import lax
from jax.sharding import PartitionSpec as P


CD_SHARES = (36, 31, 21)
LANES = 128


def cuts(length, shares, unit):
    tiles = -(-length // unit)
    edges = [tiles * sum(shares[:at]) // sum(shares) * unit for at in range(len(shares))]
    return list(zip(edges, edges[1:] + [length]))


def shards(amplitudes, coulomb):
    columns = lax.axis_size("col")
    pairs_here = amplitudes.shape[0]
    blocks = amplitudes.reshape(pairs_here, columns, -1).transpose(1, 0, 2)
    cd_cuts = cuts(coulomb.shape[0], CD_SHARES, LANES)
    total = None
    token = None
    for low, high in cd_cuts:
        piece = blocks[:, :, low:high]
        if token is not None:
            piece, token = lax.optimization_barrier((piece, token))
        mine = lax.all_to_all(piece, "col", split_axis=0, concat_axis=0, tiled=True)
        mine = mine.reshape(columns * pairs_here, -1)
        token = mine
        panel = lax.all_gather(mine, "row", axis=0, tiled=True)
        term = jnp.dot(panel, coulomb[low:high], preferred_element_type=jnp.float32)
        total = lax.optimization_barrier(term if total is None else total + term)
    return 0.5 * lax.psum_scatter(total, "col", scatter_dimension=0, tiled=True)


def solution(mesh):
    return jax.shard_map(
        shards,
        mesh=mesh,
        in_specs=(P(("row", "col"), None), P("col", "row")),
        out_specs=P("col", "row"),
        check_vma=False,
    )
```

time: 344 us -> 313 us (0.910)
  waiting for transfers between devices: 134 us -> 108 us
  matrix products: 58.5 us -> 53.2 us
    reduce_scatter x2 -> x1, waiting for transfers between devices: 116 us -> 103 us  [shards(): return 0.5 * lax.psum_scatter(total, 'col', scatter_dimension=0, tiled=True)]
    all_gather x3, waiting for transfers between devices: 17.6 us -> 4.47 us  [shards(): panel = lax.all_gather(mine, 'row', axis=0, tiled=True)]
    dot_general x6 -> x3, matrix products: 58.5 us -> 53.2 us  [shards(): term = jnp.dot(panel, coulomb[low:high], preferred_element_type=jnp.float32)]
  transfers between devices with their start and end apart: 5 -> 4, of which waited for: 3 -> 2; matrix products, arithmetic and copies ran while one was open for 15% -> 14% of each run, Pallas kernels for 0% -> 0%
where the time goes in v3:
time: 313 us
  blocking collectives  116 us (37%)
  waiting for transfers between devices  108 us (35%)
  matrix products  53.2 us (17%)
  local copies, waits for them, and re-layouts  20.4 us (7%)
  between operations  13.2 us (4%)
    all_to_all x3, blocking collectives, shards(): mine = lax.all_to_all(piece, 'col', split_axis=0, concat_axis=0, tiled=True)  116 us
    reduce_scatter x1, waiting for transfers between devices, shards(): return 0.5 * lax.psum_scatter(total, 'col', scatter_dimension=0, tiled=True)  103 us
    dot_general x3, matrix products, shards(): term = jnp.dot(panel, coulomb[low:high], preferred_element_type=jnp.float32)  53.2 us
    reshape x2, local copies, waits for them, and re-layouts, shards(): blocks = amplitudes.reshape(pairs_here, columns, -1).transpose(1, 0, 2)  11.6 us
  transfers between devices with their start and end apart: 4, of which 2 were waited for; matrix products, arithmetic and copies ran while one was open for 14% of the time, Pallas kernels for 0%

profile of v3, /device:TPU:0, one launch (start us, length us, event | category | flops | bytes accessed | tf_op | source)
XLA Modules:
  0.0 312.5 jit_solution(7985865079710919562)
XLA Ops:
  6.5 0.0 all-gather.4.cloned.1.call-start
  6.5 7.6 %reshape.12 = bf16[20,8,11250]{2,1,0:T(8,128)(2,1)} reshape(bf16[20,90000]{1,0:T(8,128)(2,1)} %param.2) | data formatting | bytes 7200000 | tf_op jit(solution)/shard_map/reshape | solution.py:20
  14.1 4.0 %copy.5 = bf16[20,8,11250]{2,0,1:T(8,128)(2,1)S(1)} copy(bf16[20,8,11250]{2,1,0:T(8,128)(2,1)} %reshape.12) | data formatting | bytes 7200000 | tf_op jit(solution)/shard_map/reshape | solution.py:20
  18.2 0.0 copy-start
  18.2 2.0 copy-done
  20.2 0.1 slice.24
  20.3 48.4 %all_to_all.15 = bf16[8,20,4608]{2,1,0:T(8,128)(2,1)S(1)} all-to-all(bf16[8,20,4608]{2,1,0:T(8,128)(2,1)S(1)} %slice.24), channel_id=1, replica_groups=mesh['row'=4,'col'=8] {'col'}, dimensions={0} | all-to-all | bytes 2949120 | tf_op jit(solution)/shard_map/all_to_all | solution.py:28
  68.7 1.3 reshape.13
  70.0 0.0 all-gather.4.cloned.1.call-update
  70.0 0.0 all-gather.6.cloned.1.call-start
  70.1 1.5 slice.25
  71.6 39.1 %all_to_all.16 = bf16[8,20,3968]{2,1,0:T(8,128)(2,1)S(1)} all-to-all(bf16[8,20,3968]{2,1,0:T(8,128)(2,1)S(1)} %slice.25), channel_id=1, replica_groups=mesh['row'=4,'col'=8] {'col'}, dimensions={0} | all-to-all | bytes 2539520 | tf_op jit(solution)/shard_map/all_to_all | solution.py:28
  110.6 1.2 reshape.14
  111.8 0.0 all-gather.6.cloned.1.call-update
  111.8 0.0 all-gather.8.cloned.1.call-start
  111.9 1.4 slice.26
  113.3 28.4 %all_to_all.17 = bf16[8,20,2674]{2,1,0:T(8,128)(2,1)S(1)} all-to-all(bf16[8,20,2674]{2,1,0:T(8,128)(2,1)S(1)} %slice.26), channel_id=1, replica_groups=mesh['row'=4,'col'=8] {'col'}, dimensions={0} | all-to-all | bytes 1711360 | tf_op jit(solution)/shard_map/all_to_all | solution.py:28
  141.7 1.3 reshape.15
  143.0 0.0 all-gather.8.cloned.1.call-update
  143.0 0.2 reduce-scatter.2.cloned.1.call-start
  143.2 0.0 all-gather.4.cloned.1.call-done
  143.2 19.5 %fusion = f32[640,2048]{1,0:T(8,128)} fusion(bf16[640,4608]{1,0:T(8,128)(2,1)} %all-gather.4.cloned.1.call-done, bf16[11250,2048]{1,0:T(8,128)(2,1)} %param.3), kind=kOutput, calls=%fused_computation | convolution fusion | flops 12079595520 | bytes 30015488 | tf_op jit(solution)/shard_map/dot_general | solution.py:32
  162.7 0.0 all-gather.6.cloned.1.call-done
  162.7 18.9 %fusion.9 = f32[640,2048]{1,0:T(8,128)} fusion(f32[640,2048]{1,0:T(8,128)} %fusion, bf16[640,3968]{1,0:T(8,128)(2,1)} %all-gather.6.cloned.1.call-done, bf16[11250,2048]{1,0:T(8,128)(2,1)} %param.3), kind=kOutput, calls=%fused_computation.8 | convolution fusion | flops 10403184640 | bytes 31817728 | tf_op jit(solution)/shard_map/dot_general | solution.py:32
  181.6 4.4 %all-gather.8.cloned.1.call-done = bf16[640,2674]{1,0:T(8,128)(2,1)} async-done(((bf16[160,2674]{1,0:T(8,128)(2,1)}), bf16[640,2674]{1,0:T(8,128)(2,1)}) %all-gather.8.cloned.1.call-update) | async-done | bytes 3422736 | tf_op jit(solution)/shard_map/all_gather | solution.py:31
  186.1 14.8 %fusion.6 = f32[640,2048]{1,0:T(8,128)} fusion(f32[640,2048]{1,0:T(8,128)} %fusion.9, bf16[640,2674]{1,0:T(8,128)(2,1)} %all-gather.8.cloned.1.call-done, bf16[11250,2048]{1,0:T(8,128)(2,1)} %param.3), kind=kOutput, calls=%fused_computation.7 | convolution fusion | flops 7011041280 | bytes 24903680 | tf_op jit(solution)/shard_map/dot_general | solution.py:32
  200.9 0.0 reduce-scatter.2.cloned.1.call-update
  200.9 103.1 %reduce-scatter.2.cloned.1.call-done = f32[80,2048]{1,0:T(8,128)} async-done(((f32[640,2048]{1,0:T(8,128)}), f32[80,2048]{1,0:T(8,128)}) %reduce-scatter.2.cloned.1.call-update) | async-done | bytes 655376 | tf_op jit(solution)/shard_map/reduce_scatter | solution.py:34
  304.0 2.0 broadcast_multiply_fusion
Async XLA Ops:
  6.5 136.7 %all-gather.4.cloned.1.call-start = ((), (), s32[]{:S(2)}) async-start(), calls=%async_computation.4 | async-start | bytes 7372800 | tf_op jit(solution)/shard_map/all_gather | solution.py:31
  18.2 2.0 copy-start
  70.0 92.7 %all-gather.6.cloned.1.call-start = ((), (), s32[]{:S(2)}) async-start(), calls=%async_computation.5 | async-start | bytes 6348800 | tf_op jit(solution)/shard_map/all_gather | solution.py:31
  111.8 74.2 %all-gather.8.cloned.1.call-start = ((), (), s32[]{:S(2)}) async-start(), calls=%async_computation.6 | async-start | bytes 4300800 | tf_op jit(solution)/shard_map/all_gather | solution.py:31
  143.0 161.1 %reduce-scatter.2.cloned.1.call-start = ((), (), s32[]{:S(2)}) async-start(), calls=%async_computation.7 | async-start | bytes 5898240 | tf_op jit(solution)/shard_map/reduce_scatter | solution.py:34
Sparse Core Ops, SparseCore 0:
  70.1 43.0 all-gather.3
  114.8 39.4 all-gather.5
  155.9 30.1 all-gather.7
  201.0 102.9 reduce-scatter.1
